TPU v7x, 512 devices: a whole 4x4x16 slice. The times are simulated.
512 devices in a mesh: seq: 128 (over x, z_lo, y, core), head: 4 (over z_hi).
Axes of the slice: x: 4, y: 4, z: 16 (z_hi: 4, z_lo: 4; z = z_hi * 4 + z_lo), core: 2. Of those that a mesh axis runs over, the one named last changes fastest.
Arguments:
- query_rows: bfloat16 [65536, 2048], P('seq', 'head'), may hold values from -18 to 18
- key_rows: bfloat16 [65536, 2048], P('seq', 'head'), may hold values from -18 to 18
- value_rows: bfloat16 [65536, 2048], P('seq', 'head'), may hold values from -6 to 6
- out_grad: bfloat16 [65536, 4096], P('seq', 'head'), may hold values from -6 to 6
- out_weight: bfloat16 [2048, 4096], P('head', 'seq'), may hold values from -0.09375 to 0.09375
Outputs:
- attended: bfloat16 [65536, 2048], P('seq', 'head')
- query_grad: bfloat16 [65536, 2048], P('seq', 'head')
- key_grad: bfloat16 [65536, 2048], P('seq', 'head')
- value_grad: bfloat16 [65536, 2048], P('seq', 'head')
All inputs are finite; a program needn't handle non-finite values.
Results may differ from a plain program's by a relative error of at most 0.0067.
Values may be sent and summed in bfloat16 or wider, within the bound.
No kernel may reach another device: no remote copies, remote signals or barrier semaphores. Data moves between devices by JAX's collectives and lax.ppermute only.
A program may use at most 64 MiB of HBM per device.

v0:
```python
import jax
import jax.numpy as jnp
from jax import lax
from jax.sharding import PartitionSpec as P

DH = 128
BLOCK = 128
SENTINEL = -1e30


def part_forward(queries, keys_part, values_part, visible, scaling, layout_forms):
    query_form, key_form, score_form, row_order, score_order = layout_forms
    scores = (
        jnp.einsum(
            query_form + "," + key_form + "->" + score_form,
            queries,
            keys_part,
            preferred_element_type=jnp.float32,
        )
        * scaling
    )
    row_max = jnp.max(jnp.where(visible, scores, SENTINEL), axis=-1)
    weights = jnp.where(visible, jnp.exp(scores - row_max[..., None]), 0.0)
    row_sum = jnp.sum(weights, axis=-1)
    partial_out = jnp.einsum(
        score_form + "," + key_form + "->" + query_form,
        weights.astype(jnp.bfloat16),
        values_part,
        preferred_element_type=jnp.float32,
    )
    return (
        scores,
        jnp.transpose(row_max, row_order),
        jnp.transpose(row_sum, row_order),
        partial_out,
    )


def part_backward(
    scores,
    visible,
    lse_rows,
    delta_rows,
    queries,
    keys_part,
    values_part,
    grad_part,
    scaling,
    layout_forms,
):
    query_form, key_form, score_form, row_order, score_order = layout_forms
    probs = jnp.where(
        visible, jnp.exp(scores - jnp.transpose(lse_rows, score_order)[..., None]), 0.0
    )
    value_part_grad = jnp.einsum(
        score_form + "," + query_form + "->" + key_form,
        probs.astype(jnp.bfloat16),
        grad_part,
        preferred_element_type=jnp.float32,
    )
    dprob = jnp.einsum(
        query_form + "," + key_form + "->" + score_form,
        grad_part,
        values_part,
        preferred_element_type=jnp.float32,
    )
    dscore = (probs * (dprob - jnp.transpose(delta_rows, score_order)[..., None])).astype(
        jnp.bfloat16
    )
    query_part_grad = (
        jnp.einsum(
            score_form + "," + key_form + "->" + query_form,
            dscore,
            keys_part,
            preferred_element_type=jnp.float32,
        )
        * scaling
    )
    key_part_grad = (
        jnp.einsum(
            score_form + "," + query_form + "->" + key_form,
            dscore,
            queries,
            preferred_element_type=jnp.float32,
        )
        * scaling
    )
    return (query_part_grad, key_part_grad, value_part_grad)


def combine_stats(max_band, sum_band, dot_band, max_strided, sum_strided, dot_strided):
    top = jnp.maximum(max_band, max_strided)
    band_factor = jnp.exp(max_band - top)
    strided_factor = jnp.exp(max_strided - top)
    total = band_factor * sum_band + strided_factor * sum_strided
    delta = (band_factor * dot_band + strided_factor * dot_strided) / total
    return (band_factor, strided_factor, total, top + jnp.log(total), delta)


def local(query_rows, key_rows, value_rows, out_grad, out_weight):
    tokens_here, width_here = query_rows.shape
    heads_here = width_here // DH
    groups = lax.axis_size("seq")
    residues = tokens_here // groups
    blocks_here = tokens_here // BLOCK
    scaling = DH ** (-0.5)
    band_forms = ("bihd", "bjhd", "bhij", (0, 2, 1), (0, 2, 1))
    strided_forms = ("ishd", "jshd", "shij", (2, 0, 1), (1, 2, 0))
    band_rows = lax.broadcasted_iota(jnp.int32, (BLOCK, BLOCK), 0)
    band_cols = lax.broadcasted_iota(jnp.int32, (BLOCK, BLOCK), 1)
    band_visible = band_cols <= band_rows
    far_rows = lax.broadcasted_iota(jnp.int32, (groups, groups), 0)
    far_cols = lax.broadcasted_iota(jnp.int32, (groups, groups), 1)
    strided_visible = far_cols < far_rows

    def band_view(values):
        return values.reshape(blocks_here, BLOCK, heads_here, DH)

    def group_view(values):
        return values.reshape(groups, residues, width_here)

    def strided_view(values):
        return values.reshape(groups, residues, heads_here, DH)

    full_grad = lax.all_gather(out_grad, "head", axis=1, tiled=True)
    grad_rows = lax.dot_general(
        full_grad,
        lax.all_gather(out_weight, "seq", axis=1, tiled=True),
        (((1,), (1,)), ((), ())),
        preferred_element_type=jnp.float32,
    ).astype(jnp.bfloat16)
    strided_query, strided_key, strided_value, strided_grad = (
        lax.all_to_all(group_view(query_rows), "seq", split_axis=0, concat_axis=0, tiled=True),
        lax.all_to_all(group_view(key_rows), "seq", split_axis=0, concat_axis=0, tiled=True),
        lax.all_to_all(group_view(value_rows), "seq", split_axis=0, concat_axis=0, tiled=True),
        lax.all_to_all(group_view(grad_rows), "seq", split_axis=0, concat_axis=0, tiled=True),
    )
    query_band = band_view(query_rows)
    key_band = band_view(key_rows)
    value_band = band_view(value_rows)
    band_scores, max_band, sum_band, out_band = part_forward(
        query_band, key_band, value_band, band_visible, scaling, band_forms
    )
    max_band = max_band.reshape(tokens_here, heads_here)
    sum_band = sum_band.reshape(tokens_here, heads_here)
    out_band = out_band.reshape(tokens_here, heads_here, DH)
    grad_heads = grad_rows.reshape(tokens_here, heads_here, DH)
    dot_band = jnp.sum(grad_heads.astype(jnp.float32) * out_band, axis=-1)
    far_query = strided_view(strided_query)
    far_key = strided_view(strided_key)
    far_value = strided_view(strided_value)
    far_scores, max_far, sum_far, out_far = part_forward(
        far_query, far_key, far_value, strided_visible, scaling, strided_forms
    )
    max_band_split = max_band.reshape(groups, residues, heads_here)
    sum_band_split = sum_band.reshape(groups, residues, heads_here)
    dot_band_split = dot_band.reshape(groups, residues, heads_here)
    home_out, home_max, home_sum, band_max_far, band_sum_far, band_dot_far = (
        lax.all_to_all(out_far, "seq", split_axis=0, concat_axis=0, tiled=True),
        lax.all_to_all(max_far, "seq", split_axis=0, concat_axis=0, tiled=True),
        lax.all_to_all(sum_far, "seq", split_axis=0, concat_axis=0, tiled=True),
        lax.all_to_all(max_band_split, "seq", split_axis=0, concat_axis=0, tiled=True),
        lax.all_to_all(sum_band_split, "seq", split_axis=0, concat_axis=0, tiled=True),
        lax.all_to_all(dot_band_split, "seq", split_axis=0, concat_axis=0, tiled=True),
    )
    home_out = home_out.reshape(tokens_here, heads_here, DH)
    home_max = home_max.reshape(tokens_here, heads_here)
    home_sum = home_sum.reshape(tokens_here, heads_here)
    home_dot = jnp.sum(grad_heads.astype(jnp.float32) * home_out, axis=-1)
    band_factor, far_factor, total, lse_home, delta_home = combine_stats(
        max_band, sum_band, dot_band, home_max, home_sum, home_dot
    )
    attended = (
        ((band_factor[..., None] * out_band + far_factor[..., None] * home_out) / total[..., None])
        .astype(jnp.bfloat16)
        .reshape(tokens_here, width_here)
    )
    far_grad = strided_view(strided_grad)
    far_dot = jnp.sum(far_grad.astype(jnp.float32) * out_far, axis=-1)
    far_stats = combine_stats(band_max_far, band_sum_far, band_dot_far, max_far, sum_far, far_dot)
    band_grads = part_backward(
        band_scores,
        band_visible,
        lse_home.reshape(blocks_here, BLOCK, heads_here),
        delta_home.reshape(blocks_here, BLOCK, heads_here),
        query_band,
        key_band,
        value_band,
        band_view(grad_rows),
        scaling,
        band_forms,
    )
    far_grads = part_backward(
        far_scores,
        strided_visible,
        far_stats[3],
        far_stats[4],
        far_query,
        far_key,
        far_value,
        far_grad,
        scaling,
        strided_forms,
    )
    home_query, home_key, home_value = (
        lax.all_to_all(
            far_grads[0].astype(jnp.bfloat16).reshape(groups, residues, width_here),
            "seq",
            split_axis=0,
            concat_axis=0,
            tiled=True,
        ),
        lax.all_to_all(
            far_grads[1].astype(jnp.bfloat16).reshape(groups, residues, width_here),
            "seq",
            split_axis=0,
            concat_axis=0,
            tiled=True,
        ),
        lax.all_to_all(
            far_grads[2].astype(jnp.bfloat16).reshape(groups, residues, width_here),
            "seq",
            split_axis=0,
            concat_axis=0,
            tiled=True,
        ),
    )
    query_grad = (
        band_grads[0].reshape(tokens_here, width_here)
        + home_query.reshape(tokens_here, width_here).astype(jnp.float32)
    ).astype(jnp.bfloat16)
    key_grad = (
        band_grads[1].reshape(tokens_here, width_here)
        + home_key.reshape(tokens_here, width_here).astype(jnp.float32)
    ).astype(jnp.bfloat16)
    value_grad = (
        band_grads[2].reshape(tokens_here, width_here)
        + home_value.reshape(tokens_here, width_here).astype(jnp.float32)
    ).astype(jnp.bfloat16)
    return (attended, query_grad, key_grad, value_grad)


def solution(mesh):
    placed = (
        P("seq", "head"),
        P("seq", "head"),
        P("seq", "head"),
        P("seq", "head"),
        P("head", "seq"),
    )
    return jax.shard_map(
        local,
        mesh=mesh,
        in_specs=placed,
        out_specs=(P("seq", "head"), P("seq", "head"), P("seq", "head"), P("seq", "head")),
        check_vma=False,
    )
```

profile of v0, /device:TPU:1, one launch (start us, length us, event | category | flops | bytes accessed | tf_op | source)
XLA Modules:
  0.0 643.3 jit_solution(7288752029031276424)
XLA Ops:
  13.1 13.8 %all-to-all-start.7 = ((f32[128,4,4]{1,2,0:T(4,128)}), f32[128,4,4]{1,2,0:T(4,128)S(1)}, u32[]{:S(2)}, u32[]{:S(2)}) async-start(f32[128,4,4]{1,2,0:T(4,128)} %copy.166), calls=%async_computation.7 | async-start | bytes 524288 | tf_op jit(solution)/shard_map/all_to_all | solution.py:163
  29.8 10.4 %all-to-all-done.7 = f32[128,4,4]{1,2,0:T(4,128)S(1)} async-done(((f32[128,4,4]{1,2,0:T(4,128)}), f32[128,4,4]{1,2,0:T(4,128)S(1)}, u32[]{:S(2)}, u32[]{:S(2)}) %all-to-all-start.7) | async-done | bytes 8224 | tf_op jit(solution)/shard_map/all_to_all | solution.py:163
  40.2 6.8 %all-to-all-start.6 = ((f32[128,4,4]{1,2,0:T(4,128)}), f32[128,4,4]{1,2,0:T(4,128)}, u32[]{:S(2)}, u32[]{:S(2)}) async-start(f32[128,4,4]{1,2,0:T(4,128)} %copy.162), calls=%async_computation.6 | async-start | bytes 524288 | tf_op jit(solution)/shard_map/all_to_all | solution.py:162
  47.9 87.7 %all-to-all-done.6 = f32[128,4,4]{1,2,0:T(4,128)} async-done(((f32[128,4,4]{1,2,0:T(4,128)}), f32[128,4,4]{1,2,0:T(4,128)}, u32[]{:S(2)}, u32[]{:S(2)}) %all-to-all-start.6) | async-done | bytes 8224 | tf_op jit(solution)/shard_map/all_to_all | solution.py:162
  135.6 6.7 %all-to-all-start = ((bf16[128,4,512]{2,1,0:T(4,128)(2,1)}), bf16[128,4,512]{2,1,0:T(4,128)(2,1)S(1)}, u32[]{:S(2)}, u32[]{:S(2)}) async-start(bf16[128,4,512]{2,1,0:T(4,128)(2,1)} %reshape.175), calls=%async_computation | async-start | bytes 1048576 | tf_op jit(solution)/shard_map/all_to_all | solution.py:133
  143.2 49.3 %all-to-all-done = bf16[128,4,512]{2,1,0:T(4,128)(2,1)S(1)} async-done(((bf16[128,4,512]{2,1,0:T(4,128)(2,1)}), bf16[128,4,512]{2,1,0:T(4,128)(2,1)S(1)}, u32[]{:S(2)}, u32[]{:S(2)}) %all-to-all-start) | async-done | bytes 524320 | tf_op jit(solution)/shard_map/all_to_all | solution.py:133
  192.5 5.9 all-to-all-start.1
  199.4 17.4 %all-to-all-done.1 = bf16[128,4,512]{2,1,0:T(4,128)(2,1)S(1)} async-done(((bf16[128,4,512]{2,1,0:T(4,128)(2,1)}), bf16[128,4,512]{2,1,0:T(4,128)(2,1)S(1)}, u32[]{:S(2)}, u32[]{:S(2)}) %all-to-all-start.1) | async-done | bytes 524320 | tf_op jit(solution)/shard_map/all_to_all | solution.py:134
  216.8 8.1 %all-to-all-start.3 = ((bf16[128,4,512]{2,1,0:T(4,128)(2,1)}), bf16[128,4,512]{2,1,0:T(4,128)(2,1)}, u32[]{:S(2)}, u32[]{:S(2)}) async-start(bf16[128,4,512]{2,1,0:T(4,128)(2,1)} %reshape.182), calls=%async_computation.3 | async-start | bytes 1048576 | tf_op jit(solution)/shard_map/all_to_all | solution.py:135
  225.1 176.4 %all-gather.5.cloned.1.call-done = bf16[512,4096]{0,1:T(8,128)(2,1)} async-done(((bf16[512,32]{0,1:T(8,128)(2,1)}), bf16[512,4096]{0,1:T(8,128)(2,1)}) %all-gather.5.cloned.1.call-update) | async-done | bytes 4194320 | tf_op jit(solution)/shard_map/all_gather | solution.py:128
  401.5 5.8 convolution_convert_fusion.1
  413.9 8.6 %all-to-all-start.9 = ((f32[128,4,4]{1,2,0:T(4,128)}), f32[128,4,4]{1,2,0:T(4,128)}, u32[]{:S(2)}, u32[]{:S(2)}) async-start(f32[128,4,4]{1,2,0:T(4,128)} %copy.172), calls=%async_computation.9 | async-start | bytes 524288 | tf_op jit(solution)/shard_map/all_to_all | solution.py:164
  423.4 11.9 %all-to-all-done.9 = f32[128,4,4]{1,2,0:T(4,128)} async-done(((f32[128,4,4]{1,2,0:T(4,128)}), f32[128,4,4]{1,2,0:T(4,128)}, u32[]{:S(2)}, u32[]{:S(2)}) %all-to-all-start.9) | async-done | bytes 8224 | tf_op jit(solution)/shard_map/all_to_all | solution.py:164
  435.4 6.9 %all-to-all-start.8 = ((bf16[128,4,512]{2,1,0:T(4,128)(2,1)}), bf16[128,4,512]{2,1,0:T(4,128)(2,1)}, u32[]{:S(2)}, u32[]{:S(2)}) async-start(bf16[128,4,512]{2,1,0:T(4,128)(2,1)} %reshape.191), calls=%async_computation.8 | async-start | bytes 1048576 | tf_op jit(solution)/shard_map/all_to_all | solution.py:136
  451.9 8.3 %all-to-all-done.8 = bf16[128,4,512]{2,1,0:T(4,128)(2,1)} async-done(((bf16[128,4,512]{2,1,0:T(4,128)(2,1)}), bf16[128,4,512]{2,1,0:T(4,128)(2,1)}, u32[]{:S(2)}, u32[]{:S(2)}) %all-to-all-start.8) | async-done | bytes 524320 | tf_op jit(solution)/shard_map/all_to_all | solution.py:136
  460.2 6.4 all-to-all-start.5
  470.4 9.5 %all-to-all-done.5 = f32[128,4,4]{1,2,0:T(4,128)S(1)} async-done(((f32[128,4,4]{1,2,0:T(4,128)}), f32[128,4,4]{1,2,0:T(4,128)S(1)}, u32[]{:S(2)}, u32[]{:S(2)}) %all-to-all-start.5) | async-done | bytes 8224 | tf_op jit(solution)/shard_map/all_to_all | solution.py:161
  479.9 7.0 %all-to-all-start.2 = ((f32[128,4,4]{1,2,0:T(4,128)}), f32[128,4,4]{1,2,0:T(4,128)}, u32[]{:S(2)}, u32[]{:S(2)}) async-start(f32[128,4,4]{1,2,0:T(4,128)} %copy.132), calls=%async_computation.2 | async-start | bytes 524288 | tf_op jit(solution)/shard_map/all_to_all | solution.py:160
  490.4 9.4 %all-to-all-done.2 = f32[128,4,4]{1,2,0:T(4,128)} async-done(((f32[128,4,4]{1,2,0:T(4,128)}), f32[128,4,4]{1,2,0:T(4,128)}, u32[]{:S(2)}, u32[]{:S(2)}) %all-to-all-start.2) | async-done | bytes 8224 | tf_op jit(solution)/shard_map/all_to_all | solution.py:160
  499.9 6.9 %all-to-all-start.12 = ((bf16[128,4,512]{2,1,0:T(4,128)(2,1)}), bf16[128,4,512]{2,1,0:T(4,128)(2,1)}, u32[]{:S(2)}, u32[]{:S(2)}) async-start(bf16[128,4,512]{2,1,0:T(4,128)(2,1)} %copy.186), calls=%async_computation.12 | async-start | bytes 1048576 | tf_op jit(solution)/shard_map/all_to_all | solution.py:220
  511.8 12.9 %all-to-all-done.12 = bf16[128,4,512]{2,1,0:T(4,128)(2,1)} async-done(((bf16[128,4,512]{2,1,0:T(4,128)(2,1)}), bf16[128,4,512]{2,1,0:T(4,128)(2,1)}, u32[]{:S(2)}, u32[]{:S(2)}) %all-to-all-start.12) | async-done | bytes 524320 | tf_op jit(solution)/shard_map/all_to_all | solution.py:220
  524.7 7.5 %all-to-all-start.11 = ((bf16[128,4,512]{2,1,0:T(4,128)(2,1)}), bf16[128,4,512]{2,1,0:T(4,128)(2,1)}, u32[]{:S(2)}, u32[]{:S(2)}) async-start(bf16[128,4,512]{2,1,0:T(4,128)(2,1)} %copy.181), calls=%async_computation.11 | async-start | bytes 1048576 | tf_op jit(solution)/shard_map/all_to_all | solution.py:213
  534.9 15.3 %all-to-all-done.11 = bf16[128,4,512]{2,1,0:T(4,128)(2,1)} async-done(((bf16[128,4,512]{2,1,0:T(4,128)(2,1)}), bf16[128,4,512]{2,1,0:T(4,128)(2,1)}, u32[]{:S(2)}, u32[]{:S(2)}) %all-to-all-start.11) | async-done | bytes 524320 | tf_op jit(solution)/shard_map/all_to_all | solution.py:213
  550.1 7.5 %all-to-all-start.10 = ((bf16[128,4,512]{2,1,0:T(4,128)(2,1)}), bf16[128,4,512]{2,1,0:T(4,128)(2,1)}, u32[]{:S(2)}, u32[]{:S(2)}) async-start(bf16[128,4,512]{2,1,0:T(4,128)(2,1)} %copy.176), calls=%async_computation.10 | async-start | bytes 1048576 | tf_op jit(solution)/shard_map/all_to_all | solution.py:206
  559.0 16.5 %all-to-all-done.10 = bf16[128,4,512]{2,1,0:T(4,128)(2,1)} async-done(((bf16[128,4,512]{2,1,0:T(4,128)(2,1)}), bf16[128,4,512]{2,1,0:T(4,128)(2,1)}, u32[]{:S(2)}, u32[]{:S(2)}) %all-to-all-start.10) | async-done | bytes 524320 | tf_op jit(solution)/shard_map/all_to_all | solution.py:206
  575.6 6.8 %all-to-all-start.4 = ((f32[128,4,4,128]{3,2,1,0:T(4,128)}), f32[128,4,4,128]{3,2,1,0:T(4,128)S(1)}, u32[]{:S(2)}, u32[]{:S(2)}) async-start(f32[128,4,4,128]{3,2,1,0:T(4,128)} %copy.141), calls=%async_computation.4 | async-start | bytes 2097152 | tf_op jit(solution)/shard_map/all_to_all | solution.py:159
  597.1 14.6 %all-to-all-done.4 = f32[128,4,4,128]{3,2,1,0:T(4,128)S(1)} async-done(((f32[128,4,4,128]{3,2,1,0:T(4,128)}), f32[128,4,4,128]{3,2,1,0:T(4,128)S(1)}, u32[]{:S(2)}, u32[]{:S(2)}) %all-to-all-start.4) | async-done | bytes 1048608 | tf_op jit(solution)/shard_map/all_to_all | solution.py:159
  611.8 2.6 multiply_reduce_fusion.1
  621.6 2.6 copy.179
  624.2 2.6 copy.160
  626.8 2.6 fusion.8
  629.4 2.6 fusion.9
  (127 shorter events, 71.3 us)
Async XLA Ops:
  7.2 217.9 %all-gather.3.cloned.1.call-start = ((), (), s32[]{:S(2)}) async-start(), calls=%async_computation.13 | async-start | bytes 5242880 | tf_op jit(solution)/shard_map/all_gather | solution.py:125
  7.9 39.1 %copy-start.11 = (bf16[512,512]{1,0:T(8,128)(2,1)S(1)}, bf16[512,512]{1,0:T(8,128)(2,1)}, u32[]{:S(2)}) copy-start(bf16[512,512]{1,0:T(8,128)(2,1)} %param.5) | copy-start | bytes 1572868
  7.9 393.6 %all-gather.5.cloned.1.call-start = ((), (), s32[]{:S(2)}) async-start(), calls=%async_computation.14 | async-start | bytes 4227072 | tf_op jit(solution)/shard_map/all_gather | solution.py:128
  11.2 132.0 %copy-start.18 = (bf16[4,128,4,128]{3,2,1,0:T(4,128)(2,1)}, bf16[4,128,4,128]{3,2,1,0:T(4,128)(2,1)S(1)}, u32[]{:S(2)}) copy-start(bf16[4,128,4,128]{3,2,1,0:T(4,128)(2,1)S(1)} %reshape.173) | copy-start | bytes 1572868
  11.2 131.1 %copy-start.12 = (bf16[512,512]{1,0:T(8,128)(2,1)S(1)}, bf16[512,512]{1,0:T(8,128)(2,1)}, u32[]{:S(2)}) copy-start(bf16[512,512]{1,0:T(8,128)(2,1)} %param.6) | copy-start | bytes 1572868
  11.8 186.7 %copy-start.13 = (bf16[512,512]{1,0:T(8,128)(2,1)S(1)}, bf16[512,512]{1,0:T(8,128)(2,1)}, u32[]{:S(2)}) copy-start(bf16[512,512]{1,0:T(8,128)(2,1)} %param.7) | copy-start | bytes 1572868
  13.1 27.0 %all-to-all-start.7 = ((f32[128,4,4]{1,2,0:T(4,128)}), f32[128,4,4]{1,2,0:T(4,128)S(1)}, u32[]{:S(2)}, u32[]{:S(2)}) async-start(f32[128,4,4]{1,2,0:T(4,128)} %copy.166), calls=%async_computation.7 | async-start | bytes 524288 | tf_op jit(solution)/shard_map/all_to_all | solution.py:163
  40.2 95.4 %all-to-all-start.6 = ((f32[128,4,4]{1,2,0:T(4,128)}), f32[128,4,4]{1,2,0:T(4,128)}, u32[]{:S(2)}, u32[]{:S(2)}) async-start(f32[128,4,4]{1,2,0:T(4,128)} %copy.162), calls=%async_computation.6 | async-start | bytes 524288 | tf_op jit(solution)/shard_map/all_to_all | solution.py:162
  135.6 57.0 %all-to-all-start = ((bf16[128,4,512]{2,1,0:T(4,128)(2,1)}), bf16[128,4,512]{2,1,0:T(4,128)(2,1)S(1)}, u32[]{:S(2)}, u32[]{:S(2)}) async-start(bf16[128,4,512]{2,1,0:T(4,128)(2,1)} %reshape.175), calls=%async_computation | async-start | bytes 1048576 | tf_op jit(solution)/shard_map/all_to_all | solution.py:133
  192.5 214.8 %copy-start.14 = (bf16[128,4,512]{2,1,0:T(4,128)(2,1)}, bf16[128,4,512]{2,1,0:T(4,128)(2,1)S(1)}, u32[]{:S(2)}) copy-start(bf16[128,4,512]{2,1,0:T(4,128)(2,1)S(1)} %all-to-all-done) | copy-start | bytes 1572868
  192.5 24.3 %all-to-all-start.1 = ((bf16[128,4,512]{2,1,0:T(4,128)(2,1)}), bf16[128,4,512]{2,1,0:T(4,128)(2,1)S(1)}, u32[]{:S(2)}, u32[]{:S(2)}) async-start(bf16[128,4,512]{2,1,0:T(4,128)(2,1)} %reshape.177), calls=%async_computation.1 | async-start | bytes 1048576 | tf_op jit(solution)/shard_map/all_to_all | solution.py:134
  216.8 8.3 %copy-start.16 = (bf16[128,4,512]{2,1,0:T(4,128)(2,1)}, bf16[128,4,512]{2,1,0:T(4,128)(2,1)S(1)}, u32[]{:S(2)}) copy-start(bf16[128,4,512]{2,1,0:T(4,128)(2,1)S(1)} %all-to-all-done.1) | copy-start | bytes 1572868
  216.8 197.1 %all-to-all-start.3 = ((bf16[128,4,512]{2,1,0:T(4,128)(2,1)}), bf16[128,4,512]{2,1,0:T(4,128)(2,1)}, u32[]{:S(2)}, u32[]{:S(2)}) async-start(bf16[128,4,512]{2,1,0:T(4,128)(2,1)} %reshape.182), calls=%async_computation.3 | async-start | bytes 1048576 | tf_op jit(solution)/shard_map/all_to_all | solution.py:135
  225.1 184.6 %copy-start.9 = (bf16[4,128,4,128]{3,2,1,0:T(4,128)(2,1)}, bf16[4,128,4,128]{3,2,1,0:T(4,128)(2,1)S(1)}, u32[]{:S(2)}) copy-start(bf16[4,128,4,128]{3,2,1,0:T(4,128)(2,1)S(1)} %reshape.180) | copy-start | bytes 1572868
  407.3 28.0 %copy-start = (bf16[512,512]{1,0:T(8,128)(2,1)}, bf16[512,512]{1,0:T(8,128)(2,1)S(1)}, u32[]{:S(2)}) copy-start(bf16[512,512]{1,0:T(8,128)(2,1)S(1)} %convolution_convert_fusion.1) | copy-start | bytes 1572868
  408.3 35.1 %copy-start.15 = (bf16[128,4,512]{2,1,0:T(4,128)(2,1)S(1)}, bf16[128,4,512]{2,1,0:T(4,128)(2,1)}, u32[]{:S(2)}) copy-start(bf16[128,4,512]{2,1,0:T(4,128)(2,1)} %copy-done.14) | copy-start | bytes 1572868
  411.1 33.6 %copy-start.17 = (bf16[128,4,512]{2,1,0:T(4,128)(2,1)S(1)}, bf16[128,4,512]{2,1,0:T(4,128)(2,1)}, u32[]{:S(2)}) copy-start(bf16[128,4,512]{2,1,0:T(4,128)(2,1)} %copy-done.16) | copy-start | bytes 1572868
  413.9 21.5 %all-to-all-start.9 = ((f32[128,4,4]{1,2,0:T(4,128)}), f32[128,4,4]{1,2,0:T(4,128)}, u32[]{:S(2)}, u32[]{:S(2)}) async-start(f32[128,4,4]{1,2,0:T(4,128)} %copy.172), calls=%async_computation.9 | async-start | bytes 524288 | tf_op jit(solution)/shard_map/all_to_all | solution.py:164
  435.4 24.8 %all-to-all-start.8 = ((bf16[128,4,512]{2,1,0:T(4,128)(2,1)}), bf16[128,4,512]{2,1,0:T(4,128)(2,1)}, u32[]{:S(2)}, u32[]{:S(2)}) async-start(bf16[128,4,512]{2,1,0:T(4,128)(2,1)} %reshape.191), calls=%async_computation.8 | async-start | bytes 1048576 | tf_op jit(solution)/shard_map/all_to_all | solution.py:136
  445.1 15.1 %copy-start.3 = (bf16[128,4,512]{0,2,1:T(8,128)(2,1)}, bf16[128,4,512]{0,2,1:T(8,128)(2,1)S(1)}, u32[]{:S(2)}) copy-start(bf16[128,4,512]{0,2,1:T(8,128)(2,1)S(1)} %copy.129) | copy-start | bytes 1572868
  460.2 19.7 %all-to-all-start.5 = ((f32[128,4,4]{1,2,0:T(4,128)}), f32[128,4,4]{1,2,0:T(4,128)S(1)}, u32[]{:S(2)}, u32[]{:S(2)}) async-start(f32[128,4,4]{1,2,0:T(4,128)} %copy.142), calls=%async_computation.5 | async-start | bytes 524288 | tf_op jit(solution)/shard_map/all_to_all | solution.py:161
  479.9 30.7 %copy-start.24 = (f32[128,4,4]{1,2,0:T(4,128)}, f32[128,4,4]{1,2,0:T(4,128)S(1)}, u32[]{:S(2)}) copy-start(f32[128,4,4]{1,2,0:T(4,128)S(1)} %all-to-all-done.5) | copy-start | bytes 24580
  479.9 20.0 %all-to-all-start.2 = ((f32[128,4,4]{1,2,0:T(4,128)}), f32[128,4,4]{1,2,0:T(4,128)}, u32[]{:S(2)}, u32[]{:S(2)}) async-start(f32[128,4,4]{1,2,0:T(4,128)} %copy.132), calls=%async_computation.2 | async-start | bytes 524288 | tf_op jit(solution)/shard_map/all_to_all | solution.py:160
  499.9 24.8 %all-to-all-start.12 = ((bf16[128,4,512]{2,1,0:T(4,128)(2,1)}), bf16[128,4,512]{2,1,0:T(4,128)(2,1)}, u32[]{:S(2)}, u32[]{:S(2)}) async-start(bf16[128,4,512]{2,1,0:T(4,128)(2,1)} %copy.186), calls=%async_computation.12 | async-start | bytes 1048576 | tf_op jit(solution)/shard_map/all_to_all | solution.py:220
  509.0 48.6 %copy-start.4 = (f32[128,4,4,128]{0,3,2,1:T(8,128)S(1)}, f32[128,4,4,128]{0,3,2,1:T(8,128)}, u32[]{:S(2)}) copy-start(f32[128,4,4,128]{0,3,2,1:T(8,128)} %get-tuple-element.16) | copy-start | bytes 3145732
  524.7 25.4 %all-to-all-start.11 = ((bf16[128,4,512]{2,1,0:T(4,128)(2,1)}), bf16[128,4,512]{2,1,0:T(4,128)(2,1)}, u32[]{:S(2)}, u32[]{:S(2)}) async-start(bf16[128,4,512]{2,1,0:T(4,128)(2,1)} %copy.181), calls=%async_computation.11 | async-start | bytes 1048576 | tf_op jit(solution)/shard_map/all_to_all | solution.py:213
  534.9 52.0 %copy-start.1 = (bf16[512,512]{1,0:T(8,128)(2,1)S(1)}, bf16[512,512]{1,0:T(8,128)(2,1)}, u32[]{:S(2)}) copy-start(bf16[512,512]{1,0:T(8,128)(2,1)} %copy-done) | copy-start | bytes 1572868
  550.1 25.4 %all-to-all-start.10 = ((bf16[128,4,512]{2,1,0:T(4,128)(2,1)}), bf16[128,4,512]{2,1,0:T(4,128)(2,1)}, u32[]{:S(2)}, u32[]{:S(2)}) async-start(bf16[128,4,512]{2,1,0:T(4,128)(2,1)} %copy.176), calls=%async_computation.10 | async-start | bytes 1048576 | tf_op jit(solution)/shard_map/all_to_all | solution.py:206
  575.6 36.2 %all-to-all-start.4 = ((f32[128,4,4,128]{3,2,1,0:T(4,128)}), f32[128,4,4,128]{3,2,1,0:T(4,128)S(1)}, u32[]{:S(2)}, u32[]{:S(2)}) async-start(f32[128,4,4,128]{3,2,1,0:T(4,128)} %copy.141), calls=%async_computation.4 | async-start | bytes 2097152 | tf_op jit(solution)/shard_map/all_to_all | solution.py:159
  592.8 24.1 %copy-start.10 = (bf16[4,128,4,128]{3,2,1,0:T(4,128)(2,1)S(1)}, bf16[4,128,4,128]{3,2,1,0:T(4,128)(2,1)}, u32[]{:S(2)}) copy-start(bf16[4,128,4,128]{3,2,1,0:T(4,128)(2,1)} %copy-done.9) | copy-start | bytes 1572868
  624.2 7.8 %copy-start.5 = (f32[512,512]{1,0:T(8,128)S(1)}, f32[512,512]{1,0:T(8,128)}, u32[]{:S(2)}) copy-start(f32[512,512]{1,0:T(8,128)} %reshape.200) | copy-start | bytes 3145732
  626.8 6.8 %copy-start.22 = (f32[512,4]{1,0:T(8,128)S(1)}, f32[512,4]{1,0:T(8,128)}, u32[]{:S(2)}) copy-start(f32[512,4]{1,0:T(8,128)} %copy.138) | copy-start | bytes 24580
  (8 other events, 25.8 us)
Sparse Core Ops, SparseCore 0:
  10.1 123.5 all-gather.2
  135.8 265.6 all-gather.4
where the time goes:
time: 653 us; the launch traced here: 643 us
  waiting for transfers between devices  441 us (68%)
  starting transfers between devices  98.9 us (15%)
  local copies, waits for them, and re-layouts  55.7 us (9%)
  matrix products  22.2 us (3%)
  between operations  14.7 us (2%)
  other arithmetic  10.7 us (2%)
    all_gather x1, waiting for transfers between devices, local(): lax.all_gather(out_weight, 'seq', axis=1, tiled=True)  176 us
    all_to_all x1, waiting for transfers between devices, local(): lax.all_to_all(max_band_split, 'seq', split_axis=0, concat_axis=0, tiled=...  87.7 us
    all_to_all x1, waiting for transfers between devices, local(): lax.all_to_all(group_view(query_rows), 'seq', split_axis=0, concat_axis=0...  49.3 us
    all_to_all x1, waiting for transfers between devices, local(): lax.all_to_all(group_view(key_rows), 'seq', split_axis=0, concat_axis=0,...  17.4 us
    all_to_all x1, waiting for transfers between devices, local(): lax.all_to_all(far_grads[0].astype(jnp.bfloat16).reshape(groups, residues...  16.5 us
    all_to_all x1, waiting for transfers between devices, local(): lax.all_to_all(far_grads[1].astype(jnp.bfloat16).reshape(groups, residues...  15.3 us
    all_to_all x1, waiting for transfers between devices, local(): lax.all_to_all(out_far, 'seq', split_axis=0, concat_axis=0, tiled=True)  14.6 us
    all_to_all x1, starting transfers between devices, local(): lax.all_to_all(sum_band_split, 'seq', split_axis=0, concat_axis=0, tiled=...  13.8 us
  transfers between devices with their start and end apart: 15, of which 13 were waited for; matrix products, arithmetic and copies ran while one was open for 10% of the time, Pallas kernels for 0%

commit v1 on v0

--- a/solution.py
+++ b/solution.py
@@ -125,7 +125,9 @@
     full_grad = lax.all_gather(out_grad, "head", axis=1, tiled=True)
     grad_rows = lax.dot_general(
         full_grad,
-        lax.all_gather(out_weight, "seq", axis=1, tiled=True),
+        jnp.concatenate(
+            lax.all_to_all(jnp.stack([out_weight] * lax.axis_size("seq")), "seq", 0, 0), axis=1
+        ),
         (((1,), (1,)), ((), ())),
         preferred_element_type=jnp.float32,
     ).astype(jnp.bfloat16)

time: 653 us -> 613 us (0.939)
  waiting for transfers between devices: 441 us -> 375 us
  blocking collectives: 0 us -> 24.8 us
    all_to_all x1, waiting for transfers between devices: 17.4 us -> 230 us  [local(): lax.all_to_all(jnp.stack([out_weight] * lax.axis_size('seq')), 'seq', 0, 0)]
    all_gather x1 -> x0, waiting for transfers between devices: 176 us -> none  [local(): lax.all_gather(out_weight, 'seq', axis=1, tiled=True)]
    all_to_all x1, waiting for transfers between devices: 87.7 us -> 11.9 us  [local(): lax.all_to_all(max_band_split, 'seq', split_axis=0, concat_axis=0, tiled=...]
    all_to_all x1, waiting for transfers between devices: 49.3 us -> 18.1 us  [local(): lax.all_to_all(group_view(query_rows), 'seq', split_axis=0, concat_axis=0...]
    all_to_all x0 -> x1, blocking collectives: none -> 24.8 us  [local(): lax.all_to_all(group_view(key_rows), 'seq', split_axis=0, concat_axis=0,...]
  transfers between devices with their start and end apart: 15 -> 14, of which waited for: 13 -> 13; matrix products, arithmetic and copies ran while one was open for 10% -> 10% of each run, Pallas kernels for 0% -> 0%
where the time goes in v1:
time: 613 us; the launch traced here: 603 us
  waiting for transfers between devices  375 us (61%)
  starting transfers between devices  98.5 us (16%)
  local copies, waits for them, and re-layouts  57.4 us (9%)
  blocking collectives  24.8 us (4%)
  matrix products  22.3 us (4%)
  between operations  14.7 us (2%)
  other arithmetic  10.7 us (2%)
    all_to_all x1, waiting for transfers between devices, local(): lax.all_to_all(jnp.stack([out_weight] * lax.axis_size('seq')), 'seq', 0, 0)  230 us
    all_to_all x1, blocking collectives, local(): lax.all_to_all(group_view(key_rows), 'seq', split_axis=0, concat_axis=0,...  24.8 us
    all_to_all x1, waiting for transfers between devices, local(): lax.all_to_all(group_view(query_rows), 'seq', split_axis=0, concat_axis=0...  18.1 us
    all_to_all x1, waiting for transfers between devices, local(): lax.all_to_all(far_grads[0].astype(jnp.bfloat16).reshape(groups, residues...  16.5 us
    all_to_all x1, waiting for transfers between devices, local(): lax.all_to_all(far_grads[1].astype(jnp.bfloat16).reshape(groups, residues...  15.3 us
    all_to_all x1, waiting for transfers between devices, local(): lax.all_to_all(out_far, 'seq', split_axis=0, concat_axis=0, tiled=True)  14.8 us
    all_to_all x1, starting transfers between devices, local(): lax.all_to_all(sum_band_split, 'seq', split_axis=0, concat_axis=0, tiled=...  13.8 us
    all_to_all x1, waiting for transfers between devices, local(): lax.all_to_all(far_grads[2].astype(jnp.bfloat16).reshape(groups, residues...  12.9 us
  transfers between devices with their start and end apart: 14, of which 13 were waited for; matrix products, arithmetic and copies ran while one was open for 10% of the time, Pallas kernels for 0%

profile of v1, /device:TPU:1, one launch (start us, length us, event | category | flops | bytes accessed | tf_op | source)
XLA Modules:
  0.0 603.3 jit_solution(8393834832992606452)
XLA Ops:
  11.7 13.8 %all-to-all-start.8 = ((f32[128,4,4]{1,2,0:T(4,128)}), f32[128,4,4]{1,2,0:T(4,128)S(1)}, u32[]{:S(2)}, u32[]{:S(2)}) async-start(f32[128,4,4]{1,2,0:T(4,128)} %copy.167), calls=%async_computation.8 | async-start | bytes 524288 | tf_op jit(solution)/shard_map/all_to_all | solution.py:165
  28.3 10.4 %all-to-all-done.8 = f32[128,4,4]{1,2,0:T(4,128)S(1)} async-done(((f32[128,4,4]{1,2,0:T(4,128)}), f32[128,4,4]{1,2,0:T(4,128)S(1)}, u32[]{:S(2)}, u32[]{:S(2)}) %all-to-all-start.8) | async-done | bytes 8224 | tf_op jit(solution)/shard_map/all_to_all | solution.py:165
  38.7 6.9 %all-to-all-start.7 = ((f32[128,4,4]{1,2,0:T(4,128)}), f32[128,4,4]{1,2,0:T(4,128)}, u32[]{:S(2)}, u32[]{:S(2)}) async-start(f32[128,4,4]{1,2,0:T(4,128)} %copy.163), calls=%async_computation.7 | async-start | bytes 524288 | tf_op jit(solution)/shard_map/all_to_all | solution.py:164
  46.5 11.9 %all-to-all-done.7 = f32[128,4,4]{1,2,0:T(4,128)} async-done(((f32[128,4,4]{1,2,0:T(4,128)}), f32[128,4,4]{1,2,0:T(4,128)}, u32[]{:S(2)}, u32[]{:S(2)}) %all-to-all-start.7) | async-done | bytes 8224 | tf_op jit(solution)/shard_map/all_to_all | solution.py:164
  58.4 6.0 all-to-all-start
  64.6 18.1 %all-to-all-done = bf16[128,4,512]{2,1,0:T(4,128)(2,1)S(1)} async-done(((bf16[128,4,512]{2,1,0:T(4,128)(2,1)}), bf16[128,4,512]{2,1,0:T(4,128)(2,1)S(1)}, u32[]{:S(2)}, u32[]{:S(2)}) %all-to-all-start) | async-done | bytes 524320 | tf_op jit(solution)/shard_map/all_to_all | solution.py:135
  82.6 24.8 %all_to_all.70 = bf16[128,4,512]{2,1,0:T(4,128)(2,1)} all-to-all(bf16[128,4,512]{2,1,0:T(4,128)(2,1)S(1)} %reshape.185), channel_id=1, replica_groups=mesh['seq'=128,'head'=4] {'seq'}, dimensions={0} | all-to-all | bytes 1048576 | tf_op jit(solution)/shard_map/all_to_all | solution.py:136
  109.9 8.2 %all-to-all-start.6 = ((bf16[128,512,32]{1,2,0:T(8,128)(2,1)}), bf16[128,512,32]{1,2,0:T(8,128)(2,1)}, u32[]{:S(2)}, u32[]{:S(2)}) async-start(bf16[128,512,32]{1,2,0:T(8,128)(2,1)} %stack.2), calls=%async_computation.6 | async-start | bytes 8388608 | tf_op jit(solution)/shard_map/all_to_all | solution.py:129
  119.7 229.8 %all-to-all-done.6 = bf16[128,512,32]{1,2,0:T(8,128)(2,1)} async-done(((bf16[128,512,32]{1,2,0:T(8,128)(2,1)}), bf16[128,512,32]{1,2,0:T(8,128)(2,1)}, u32[]{:S(2)}, u32[]{:S(2)}) %all-to-all-start.6) | async-done | bytes 4194336 | tf_op jit(solution)/shard_map/all_to_all | solution.py:129
  349.5 7.5 %all-to-all-start.3 = ((bf16[128,4,512]{2,1,0:T(4,128)(2,1)}), bf16[128,4,512]{2,1,0:T(4,128)(2,1)}, u32[]{:S(2)}, u32[]{:S(2)}) async-start(bf16[128,4,512]{2,1,0:T(4,128)(2,1)} %reshape.190), calls=%async_computation.3 | async-start | bytes 1048576 | tf_op jit(solution)/shard_map/all_to_all | solution.py:137
  357.2 5.9 convolution_convert_fusion.1
  369.6 5.4 all-to-all-done.3
  374.9 7.5 %all-to-all-start.10 = ((f32[128,4,4]{1,2,0:T(4,128)}), f32[128,4,4]{1,2,0:T(4,128)}, u32[]{:S(2)}, u32[]{:S(2)}) async-start(f32[128,4,4]{1,2,0:T(4,128)} %copy.173), calls=%async_computation.10 | async-start | bytes 524288 | tf_op jit(solution)/shard_map/all_to_all | solution.py:166
  383.3 12.0 %all-to-all-done.10 = f32[128,4,4]{1,2,0:T(4,128)} async-done(((f32[128,4,4]{1,2,0:T(4,128)}), f32[128,4,4]{1,2,0:T(4,128)}, u32[]{:S(2)}, u32[]{:S(2)}) %all-to-all-start.10) | async-done | bytes 8224 | tf_op jit(solution)/shard_map/all_to_all | solution.py:166
  395.4 6.9 %all-to-all-start.9 = ((bf16[128,4,512]{2,1,0:T(4,128)(2,1)}), bf16[128,4,512]{2,1,0:T(4,128)(2,1)}, u32[]{:S(2)}, u32[]{:S(2)}) async-start(bf16[128,4,512]{2,1,0:T(4,128)(2,1)} %reshape.201), calls=%async_computation.9 | async-start | bytes 1048576 | tf_op jit(solution)/shard_map/all_to_all | solution.py:138
  411.9 8.3 %all-to-all-done.9 = bf16[128,4,512]{2,1,0:T(4,128)(2,1)} async-done(((bf16[128,4,512]{2,1,0:T(4,128)(2,1)}), bf16[128,4,512]{2,1,0:T(4,128)(2,1)}, u32[]{:S(2)}, u32[]{:S(2)}) %all-to-all-start.9) | async-done | bytes 524320 | tf_op jit(solution)/shard_map/all_to_all | solution.py:138
  420.2 6.5 %all-to-all-start.5 = ((f32[128,4,4]{1,2,0:T(4,128)}), f32[128,4,4]{1,2,0:T(4,128)S(1)}, u32[]{:S(2)}, u32[]{:S(2)}) async-start(f32[128,4,4]{1,2,0:T(4,128)} %copy.143), calls=%async_computation.5 | async-start | bytes 524288 | tf_op jit(solution)/shard_map/all_to_all | solution.py:163
  430.5 9.5 %all-to-all-done.5 = f32[128,4,4]{1,2,0:T(4,128)S(1)} async-done(((f32[128,4,4]{1,2,0:T(4,128)}), f32[128,4,4]{1,2,0:T(4,128)S(1)}, u32[]{:S(2)}, u32[]{:S(2)}) %all-to-all-start.5) | async-done | bytes 8224 | tf_op jit(solution)/shard_map/all_to_all | solution.py:163
  440.0 6.9 %all-to-all-start.2 = ((f32[128,4,4]{1,2,0:T(4,128)}), f32[128,4,4]{1,2,0:T(4,128)}, u32[]{:S(2)}, u32[]{:S(2)}) async-start(f32[128,4,4]{1,2,0:T(4,128)} %copy.133), calls=%async_computation.2 | async-start | bytes 524288 | tf_op jit(solution)/shard_map/all_to_all | solution.py:162
  450.4 9.4 %all-to-all-done.2 = f32[128,4,4]{1,2,0:T(4,128)} async-done(((f32[128,4,4]{1,2,0:T(4,128)}), f32[128,4,4]{1,2,0:T(4,128)}, u32[]{:S(2)}, u32[]{:S(2)}) %all-to-all-start.2) | async-done | bytes 8224 | tf_op jit(solution)/shard_map/all_to_all | solution.py:162
  459.9 6.8 %all-to-all-start.13 = ((bf16[128,4,512]{2,1,0:T(4,128)(2,1)}), bf16[128,4,512]{2,1,0:T(4,128)(2,1)}, u32[]{:S(2)}, u32[]{:S(2)}) async-start(bf16[128,4,512]{2,1,0:T(4,128)(2,1)} %copy.187), calls=%async_computation.13 | async-start | bytes 1048576 | tf_op jit(solution)/shard_map/all_to_all | solution.py:222
  471.8 12.9 %all-to-all-done.13 = bf16[128,4,512]{2,1,0:T(4,128)(2,1)} async-done(((bf16[128,4,512]{2,1,0:T(4,128)(2,1)}), bf16[128,4,512]{2,1,0:T(4,128)(2,1)}, u32[]{:S(2)}, u32[]{:S(2)}) %all-to-all-start.13) | async-done | bytes 524320 | tf_op jit(solution)/shard_map/all_to_all | solution.py:222
  484.7 7.5 %all-to-all-start.12 = ((bf16[128,4,512]{2,1,0:T(4,128)(2,1)}), bf16[128,4,512]{2,1,0:T(4,128)(2,1)}, u32[]{:S(2)}, u32[]{:S(2)}) async-start(bf16[128,4,512]{2,1,0:T(4,128)(2,1)} %copy.182), calls=%async_computation.12 | async-start | bytes 1048576 | tf_op jit(solution)/shard_map/all_to_all | solution.py:215
  494.8 15.3 %all-to-all-done.12 = bf16[128,4,512]{2,1,0:T(4,128)(2,1)} async-done(((bf16[128,4,512]{2,1,0:T(4,128)(2,1)}), bf16[128,4,512]{2,1,0:T(4,128)(2,1)}, u32[]{:S(2)}, u32[]{:S(2)}) %all-to-all-start.12) | async-done | bytes 524320 | tf_op jit(solution)/shard_map/all_to_all | solution.py:215
  510.1 7.7 %all-to-all-start.11 = ((bf16[128,4,512]{2,1,0:T(4,128)(2,1)}), bf16[128,4,512]{2,1,0:T(4,128)(2,1)}, u32[]{:S(2)}, u32[]{:S(2)}) async-start(bf16[128,4,512]{2,1,0:T(4,128)(2,1)} %copy.177), calls=%async_computation.11 | async-start | bytes 1048576 | tf_op jit(solution)/shard_map/all_to_all | solution.py:208
  519.2 16.5 %all-to-all-done.11 = bf16[128,4,512]{2,1,0:T(4,128)(2,1)} async-done(((bf16[128,4,512]{2,1,0:T(4,128)(2,1)}), bf16[128,4,512]{2,1,0:T(4,128)(2,1)}, u32[]{:S(2)}, u32[]{:S(2)}) %all-to-all-start.11) | async-done | bytes 524320 | tf_op jit(solution)/shard_map/all_to_all | solution.py:208
  535.8 6.4 %all-to-all-start.4 = ((f32[128,4,4,128]{3,2,1,0:T(4,128)}), f32[128,4,4,128]{3,2,1,0:T(4,128)S(1)}, u32[]{:S(2)}, u32[]{:S(2)}) async-start(f32[128,4,4,128]{3,2,1,0:T(4,128)} %copy.142), calls=%async_computation.4 | async-start | bytes 2097152 | tf_op jit(solution)/shard_map/all_to_all | solution.py:161
  556.9 14.8 %all-to-all-done.4 = f32[128,4,4,128]{3,2,1,0:T(4,128)S(1)} async-done(((f32[128,4,4,128]{3,2,1,0:T(4,128)}), f32[128,4,4,128]{3,2,1,0:T(4,128)S(1)}, u32[]{:S(2)}, u32[]{:S(2)}) %all-to-all-start.4) | async-done | bytes 1048608 | tf_op jit(solution)/shard_map/all_to_all | solution.py:161
  571.7 2.6 multiply_reduce_fusion.1
  584.2 2.7 copy.161
  586.8 2.6 fusion.8
  589.4 2.6 fusion.9
  (122 shorter events, 74.7 us)
Async XLA Ops:
  7.2 38.4 %copy-start.11 = (bf16[512,512]{1,0:T(8,128)(2,1)S(1)}, bf16[512,512]{1,0:T(8,128)(2,1)}, u32[]{:S(2)}) copy-start(bf16[512,512]{1,0:T(8,128)(2,1)} %param.5) | copy-start | bytes 1572868
  8.4 50.0 %copy-start.17 = (bf16[4,128,4,128]{3,2,1,0:T(4,128)(2,1)}, bf16[4,128,4,128]{3,2,1,0:T(4,128)(2,1)S(1)}, u32[]{:S(2)}) copy-start(bf16[4,128,4,128]{3,2,1,0:T(4,128)(2,1)S(1)} %reshape.180) | copy-start | bytes 1572868
  9.8 54.8 %copy-start.15 = (bf16[4,128,4,128]{3,2,1,0:T(4,128)(2,1)}, bf16[4,128,4,128]{3,2,1,0:T(4,128)(2,1)S(1)}, u32[]{:S(2)}) copy-start(bf16[4,128,4,128]{3,2,1,0:T(4,128)(2,1)S(1)} %reshape.181) | copy-start | bytes 1572868
  9.8 54.6 %copy-start.12 = (bf16[512,512]{1,0:T(8,128)(2,1)S(1)}, bf16[512,512]{1,0:T(8,128)(2,1)}, u32[]{:S(2)}) copy-start(bf16[512,512]{1,0:T(8,128)(2,1)} %param.6) | copy-start | bytes 1572868
  10.3 97.1 %copy-start.22 = (bf16[512,32]{0,1:T(8,128)(2,1)S(1)}, bf16[512,32]{0,1:T(8,128)(2,1)}, u32[]{:S(2)}) copy-start(bf16[512,32]{0,1:T(8,128)(2,1)} %param.9) | copy-start | bytes 98308
  11.7 27.0 %all-to-all-start.8 = ((f32[128,4,4]{1,2,0:T(4,128)}), f32[128,4,4]{1,2,0:T(4,128)S(1)}, u32[]{:S(2)}, u32[]{:S(2)}) async-start(f32[128,4,4]{1,2,0:T(4,128)} %copy.167), calls=%async_computation.8 | async-start | bytes 524288 | tf_op jit(solution)/shard_map/all_to_all | solution.py:165
  38.7 19.7 %all-to-all-start.7 = ((f32[128,4,4]{1,2,0:T(4,128)}), f32[128,4,4]{1,2,0:T(4,128)}, u32[]{:S(2)}, u32[]{:S(2)}) async-start(f32[128,4,4]{1,2,0:T(4,128)} %copy.163), calls=%async_computation.7 | async-start | bytes 524288 | tf_op jit(solution)/shard_map/all_to_all | solution.py:164
  58.4 24.2 %all-to-all-start = ((bf16[128,4,512]{2,1,0:T(4,128)(2,1)}), bf16[128,4,512]{2,1,0:T(4,128)(2,1)S(1)}, u32[]{:S(2)}, u32[]{:S(2)}) async-start(bf16[128,4,512]{2,1,0:T(4,128)(2,1)} %reshape.183), calls=%async_computation | async-start | bytes 1048576 | tf_op jit(solution)/shard_map/all_to_all | solution.py:135
  109.9 8.9 %copy-start.13 = (bf16[512,512]{1,0:T(8,128)(2,1)S(1)}, bf16[512,512]{1,0:T(8,128)(2,1)}, u32[]{:S(2)}) copy-start(bf16[512,512]{1,0:T(8,128)(2,1)} %param.7) | copy-start | bytes 1572868
  109.9 239.6 %all-to-all-start.6 = ((bf16[128,512,32]{1,2,0:T(8,128)(2,1)}), bf16[128,512,32]{1,2,0:T(8,128)(2,1)}, u32[]{:S(2)}, u32[]{:S(2)}) async-start(bf16[128,512,32]{1,2,0:T(8,128)(2,1)} %stack.2), calls=%async_computation.6 | async-start | bytes 8388608 | tf_op jit(solution)/shard_map/all_to_all | solution.py:129
  118.1 239.1 %all-gather.2.cloned.1.call-start = ((), (), s32[]{:S(2)}) async-start(), calls=%async_computation.14 | async-start | bytes 5242880 | tf_op jit(solution)/shard_map/all_gather | solution.py:125
  349.5 25.5 %all-to-all-start.3 = ((bf16[128,4,512]{2,1,0:T(4,128)(2,1)}), bf16[128,4,512]{2,1,0:T(4,128)(2,1)}, u32[]{:S(2)}, u32[]{:S(2)}) async-start(bf16[128,4,512]{2,1,0:T(4,128)(2,1)} %reshape.190), calls=%async_computation.3 | async-start | bytes 1048576 | tf_op jit(solution)/shard_map/all_to_all | solution.py:137
  357.1 8.3 %copy-start.9 = (bf16[4,128,4,128]{3,2,1,0:T(4,128)(2,1)}, bf16[4,128,4,128]{3,2,1,0:T(4,128)(2,1)S(1)}, u32[]{:S(2)}) copy-start(bf16[4,128,4,128]{3,2,1,0:T(4,128)(2,1)S(1)} %reshape.188) | copy-start | bytes 1572868
  363.1 32.3 %copy-start = (bf16[512,512]{1,0:T(8,128)(2,1)}, bf16[512,512]{1,0:T(8,128)(2,1)S(1)}, u32[]{:S(2)}) copy-start(bf16[512,512]{1,0:T(8,128)(2,1)S(1)} %convolution_convert_fusion.1) | copy-start | bytes 1572868
  366.8 37.9 %copy-start.14 = (bf16[128,4,512]{2,1,0:T(4,128)(2,1)S(1)}, bf16[128,4,512]{2,1,0:T(4,128)(2,1)}, u32[]{:S(2)}) copy-start(bf16[128,4,512]{2,1,0:T(4,128)(2,1)} %all_to_all.70) | copy-start | bytes 1572868
  374.9 20.4 %all-to-all-start.10 = ((f32[128,4,4]{1,2,0:T(4,128)}), f32[128,4,4]{1,2,0:T(4,128)}, u32[]{:S(2)}, u32[]{:S(2)}) async-start(f32[128,4,4]{1,2,0:T(4,128)} %copy.173), calls=%async_computation.10 | async-start | bytes 524288 | tf_op jit(solution)/shard_map/all_to_all | solution.py:166
  395.4 24.8 %all-to-all-start.9 = ((bf16[128,4,512]{2,1,0:T(4,128)(2,1)}), bf16[128,4,512]{2,1,0:T(4,128)(2,1)}, u32[]{:S(2)}, u32[]{:S(2)}) async-start(bf16[128,4,512]{2,1,0:T(4,128)(2,1)} %reshape.201), calls=%async_computation.9 | async-start | bytes 1048576 | tf_op jit(solution)/shard_map/all_to_all | solution.py:138
  405.1 15.1 %copy-start.3 = (bf16[128,4,512]{0,2,1:T(8,128)(2,1)}, bf16[128,4,512]{0,2,1:T(8,128)(2,1)S(1)}, u32[]{:S(2)}) copy-start(bf16[128,4,512]{0,2,1:T(8,128)(2,1)S(1)} %copy.130) | copy-start | bytes 1572868
  420.2 19.8 %all-to-all-start.5 = ((f32[128,4,4]{1,2,0:T(4,128)}), f32[128,4,4]{1,2,0:T(4,128)S(1)}, u32[]{:S(2)}, u32[]{:S(2)}) async-start(f32[128,4,4]{1,2,0:T(4,128)} %copy.143), calls=%async_computation.5 | async-start | bytes 524288 | tf_op jit(solution)/shard_map/all_to_all | solution.py:163
  440.0 30.6 %copy-start.21 = (f32[128,4,4]{1,2,0:T(4,128)}, f32[128,4,4]{1,2,0:T(4,128)S(1)}, u32[]{:S(2)}) copy-start(f32[128,4,4]{1,2,0:T(4,128)S(1)} %all-to-all-done.5) | copy-start | bytes 24580
  440.0 19.8 %all-to-all-start.2 = ((f32[128,4,4]{1,2,0:T(4,128)}), f32[128,4,4]{1,2,0:T(4,128)}, u32[]{:S(2)}, u32[]{:S(2)}) async-start(f32[128,4,4]{1,2,0:T(4,128)} %copy.133), calls=%async_computation.2 | async-start | bytes 524288 | tf_op jit(solution)/shard_map/all_to_all | solution.py:162
  459.9 24.8 %all-to-all-start.13 = ((bf16[128,4,512]{2,1,0:T(4,128)(2,1)}), bf16[128,4,512]{2,1,0:T(4,128)(2,1)}, u32[]{:S(2)}, u32[]{:S(2)}) async-start(bf16[128,4,512]{2,1,0:T(4,128)(2,1)} %copy.187), calls=%async_computation.13 | async-start | bytes 1048576 | tf_op jit(solution)/shard_map/all_to_all | solution.py:222
  469.0 48.8 %copy-start.4 = (f32[128,4,4,128]{0,3,2,1:T(8,128)S(1)}, f32[128,4,4,128]{0,3,2,1:T(8,128)}, u32[]{:S(2)}) copy-start(f32[128,4,4,128]{0,3,2,1:T(8,128)} %get-tuple-element.16) | copy-start | bytes 3145732
  484.7 25.4 %all-to-all-start.12 = ((bf16[128,4,512]{2,1,0:T(4,128)(2,1)}), bf16[128,4,512]{2,1,0:T(4,128)(2,1)}, u32[]{:S(2)}, u32[]{:S(2)}) async-start(bf16[128,4,512]{2,1,0:T(4,128)(2,1)} %copy.182), calls=%async_computation.12 | async-start | bytes 1048576 | tf_op jit(solution)/shard_map/all_to_all | solution.py:215
  494.8 51.9 %copy-start.1 = (bf16[512,512]{1,0:T(8,128)(2,1)S(1)}, bf16[512,512]{1,0:T(8,128)(2,1)}, u32[]{:S(2)}) copy-start(bf16[512,512]{1,0:T(8,128)(2,1)} %copy-done) | copy-start | bytes 1572868
  510.1 25.6 %all-to-all-start.11 = ((bf16[128,4,512]{2,1,0:T(4,128)(2,1)}), bf16[128,4,512]{2,1,0:T(4,128)(2,1)}, u32[]{:S(2)}, u32[]{:S(2)}) async-start(bf16[128,4,512]{2,1,0:T(4,128)(2,1)} %copy.177), calls=%async_computation.11 | async-start | bytes 1048576 | tf_op jit(solution)/shard_map/all_to_all | solution.py:208
  535.8 36.0 %all-to-all-start.4 = ((f32[128,4,4,128]{3,2,1,0:T(4,128)}), f32[128,4,4,128]{3,2,1,0:T(4,128)S(1)}, u32[]{:S(2)}, u32[]{:S(2)}) async-start(f32[128,4,4,128]{3,2,1,0:T(4,128)} %copy.142), calls=%async_computation.4 | async-start | bytes 2097152 | tf_op jit(solution)/shard_map/all_to_all | solution.py:161
  552.6 24.3 %copy-start.10 = (bf16[4,128,4,128]{3,2,1,0:T(4,128)(2,1)S(1)}, bf16[4,128,4,128]{3,2,1,0:T(4,128)(2,1)}, u32[]{:S(2)}) copy-start(bf16[4,128,4,128]{3,2,1,0:T(4,128)(2,1)} %copy-done.9) | copy-start | bytes 1572868
  584.2 7.9 %copy-start.5 = (f32[512,512]{1,0:T(8,128)S(1)}, f32[512,512]{1,0:T(8,128)}, u32[]{:S(2)}) copy-start(f32[512,512]{1,0:T(8,128)} %reshape.210) | copy-start | bytes 3145732
  586.8 5.2 copy-start.7
  586.8 6.8 %copy-start.19 = (f32[512,4]{1,0:T(8,128)S(1)}, f32[512,4]{1,0:T(8,128)}, u32[]{:S(2)}) copy-start(f32[512,4]{1,0:T(8,128)} %copy.139) | copy-start | bytes 24580
  589.4 5.4 copy-start.8
  (5 other events, 13.8 us)
Sparse Core Ops, SparseCore 0:
  121.0 161.9 all-gather.1
